TPU v7x, 32 devices: a whole 2x2x4 slice. The times are simulated.
32 devices in a mesh: space: 16 (over z, x, core), tm: 2 (over y).
Axes of the slice: x: 2, y: 2, z: 4, core: 2. Of those that a mesh axis runs over, the one named last changes fastest.
Arguments:
- thermal_anomaly: bfloat16 [128, 140288], P('tm', 'space'), may hold values from -6 to 6
- smoothing_coefs: float32 [128], replicated, may hold values from -0.0075 to 0.0075
Outputs:
- orthonormal_basis: float32 [128, 140288], P(None, ('space', 'tm'))
- triangular_factor: float32 [128, 128], replicated
All inputs are finite; a program needn't handle non-finite values.
Results may differ from a plain program's by a relative error of at most 0.0003.
The roundings to bfloat16 on the way count: a program that leaves them out, or rounds other values in their place, can miss the bound.
Values may be sent and summed in bfloat16 or wider, within the bound.
A program may use at most 64 MiB of HBM per device.

v0:
```python
import jax
import jax.numpy as jnp
from jax import lax
from jax.sharding import PartitionSpec as P


def shifted(block, axis, distance):
    devices = range(lax.axis_size(axis))
    route = [(i - distance, i) for i in devices if i - distance in devices]
    return lax.ppermute(block, axis, route)


def banded_matrix(coefficients, count_rows, count_cols, delay_shift_amount):
    row_index = lax.broadcasted_iota(jnp.int32, (count_rows, count_cols), 0)
    col_index = lax.broadcasted_iota(jnp.int32, (count_rows, count_cols), 1)
    lag_index = row_index + delay_shift_amount - col_index
    length = coefficients.shape[0]
    inside = (lag_index >= 0) & (lag_index < length)
    safe = jnp.clip(lag_index, 0, length - 1)
    return jnp.where(inside, coefficients[safe], jnp.zeros((), coefficients.dtype))


def product_low(left, right):
    return jnp.dot(left, right.T, preferred_element_type=jnp.float32)


def summed_gram(panel):
    width_block = panel.shape[0] // 4
    pieces = [panel[index * width_block : (index + 1) * width_block] for index in range(4)]
    listing = []
    for row_block in range(4):
        for col_block in range(row_block + 1):
            listing.append(product_low(pieces[row_block], pieces[col_block]))
    stacked = lax.psum(jnp.stack(listing), ("space", "tm"))
    lookup = {}
    position = 0
    for row_block in range(4):
        for col_block in range(row_block + 1):
            lookup[row_block, col_block] = stacked[position]
            position = position + 1
    band_rows = []
    for row_block in range(4):
        entries = []
        for col_block in range(4):
            if col_block <= row_block:
                entries.append(lookup[row_block, col_block])
            else:
                entries.append(lookup[col_block, row_block].T)
        band_rows.append(jnp.concatenate(entries, axis=1))
    return jnp.concatenate(band_rows, axis=0)


def body(thermal_anomaly, smoothing_coefs):
    timesteps_each_shard = thermal_anomaly.shape[0]
    coefficients = jnp.concatenate([jnp.ones((1,), jnp.float32), smoothing_coefs]).astype(
        jnp.bfloat16
    )
    prior_timesteps = []
    for delay_shift_amount in (2, 1):
        prior_timesteps.append(shifted(thermal_anomaly, "tm", delay_shift_amount))
    extended_record = jnp.concatenate(prior_timesteps + [thermal_anomaly], axis=0)
    snapshot_array = banded_matrix(
        coefficients, timesteps_each_shard, 3 * timesteps_each_shard, 2 * timesteps_each_shard
    )
    outgoing = jnp.dot(snapshot_array, extended_record, preferred_element_type=jnp.float32).astype(
        jnp.bfloat16
    )
    arrived = lax.all_to_all(outgoing, "tm", split_axis=1, concat_axis=0, tiled=True)
    gram = summed_gram(arrived)
    lower_one = jnp.linalg.cholesky(gram)
    first_rows = jax.scipy.linalg.solve_triangular(
        lower_one, arrived.astype(jnp.float32), lower=True
    )
    location_total = thermal_anomaly.shape[1] * lax.axis_size("space")
    scale = jnp.sqrt(jnp.float32(location_total))
    return (first_rows * scale, lower_one / scale)


def solution(mesh):
    placed = (P("tm", "space"), P())
    return jax.shard_map(
        body, mesh=mesh, in_specs=placed, out_specs=(P(None, ("space", "tm")), P()), check_vma=False
    )
```

profile of v0, /device:TPU:0, one launch (start us, length us, event | category | flops | bytes accessed | tf_op | source)
XLA Modules:
  0.0 173.4 jit_solution(4869511577980264260)
XLA Ops:
  0.6 0.7 collective-permute-start
  1.4 5.9 %collective-permute-start.1 = (bf16[64,8768]{1,0:T(8,128)(2,1)}, bf16[64,8768]{1,0:T(8,128)(2,1)}, u32[]{:S(2)}, u32[]{:S(2)}) collective-permute-start(bf16[64,8768]{1,0:T(8,128)(2,1)} %param.2), channel_id=1, source_target_pairs={{0,1},{2,3},{4,5},{6,7},{8,9},{10,11},{12,13},{14,15},{16,17},{18,... | collective-permute-start | bytes 3366920 | tf_op jit(solution)/shard_map/ppermute | solution.py:10
  7.3 0.7 convert.4
  7.9 0.1 compare_select_fusion
  8.0 0.1 reshape.58
  8.1 0.1 pad_maximum_fusion.2
  8.2 0.0 copy-start
  8.2 72.2 %gather_fusion = bf16[12288]{0:T(1024)(128)(2,1)S(1)} fusion(bf16[129]{0:T(256)(128)(2,1)S(1)} %pad_maximum_fusion.2, s32[12288]{0:T(1024)S(1)} %broadcast_clamp_fusion), kind=kCustom, calls=%fused_computation | custom fusion | bytes 98304 | tf_op jit(solution)/shard_map/gather | solution.py:20
  80.4 0.1 reshape.57
  80.5 0.0 collective-permute-done
  80.5 0.0 collective-permute-done.1
  80.5 0.0 copy-done
  80.5 2.1 %convolution_convert_fusion = bf16[64,8768]{1,0:T(8,128)(2,1)S(1)} fusion(bf16[64,8768]{1,0:T(8,128)(2,1)S(1)} %copy-done, bf16[64,8768]{1,0:T(8,128)(2,1)} %collective-permute-done.1, bf16[64,8768]{1,0:T(8,128)(2,1)S(1)} %collective-permute-done, bf16[64,192]{1,0:T(8,128)(2,1)S(1)} %reshape.57, s32[64]{0:T(128)S(1)} %iota_add_fusion), kind=kOutput, calls=%fused_computation.1 | convolution fusion | flops 226205696 | bytes 4514048 | tf_op jit(solution)/shard_map/dot_general | solution.py:65
  82.6 1.2 all_to_all.14
  83.8 0.1 copy.76
  84.0 17.1 %all_to_all.19 = bf16[64,2,4384]{2,0,1:T(8,128)(2,1)S(1)} all-to-all(bf16[64,2,4384]{2,0,1:T(8,128)(2,1)S(1)} %copy.76), channel_id=1, replica_groups=mesh['space'=16,'tm'=2] {'tm'}, dimensions={1} | all-to-all | bytes 2244608 | tf_op jit(solution)/shard_map/all_to_all | solution.py:68
  101.1 0.2 fusion.14
  101.3 0.2 fusion.13
  101.5 0.2 fusion.12
  101.7 0.2 fusion.11
  101.9 0.2 fusion.10
  102.1 0.2 fusion.9
  102.4 0.2 fusion.8
  102.6 0.2 fusion.7
  102.8 0.2 fusion.6
  103.0 0.2 fusion.5
  103.3 42.9 %psum.7 = f32[10,32,32]{1,2,0:T(8,128)S(1)} all-reduce(f32[10,32,32]{1,2,0:T(8,128)S(1)} %fusion.5), channel_id=1, replica_groups=mesh['space'=16,'tm'=2] {'space','tm'}, use_global_device_ids=true, to_apply=%region_0.1 | all-reduce | flops 10240 | bytes 81920 | tf_op jit(solution)/shard_map/psum | solution.py:34
  146.2 0.1 copy.106
  146.2 0.1 copy.107
  146.3 0.1 copy.108
  146.4 0.1 copy.91
  146.4 0.1 copy.109
  146.5 0.1 pad_maximum_fusion
  146.6 0.1 copy.93
  146.7 0.1 copy.94
  146.8 0.1 maximum_maximum_fusion
  147.0 0.1 copy.95
  147.1 0.1 fusion.32
  147.2 11.7 %cholesky.16 = f32[128,128]{1,0:T(8,128)S(1)} custom-call(f32[128,128]{1,0:T(8,128)S(1)} %fusion.32), custom_call_target="Cholesky" | custom-call | tf_op jit(solution)/shard_map/jit(cholesky)/cholesky | solution.py:70
  158.9 0.6 compare_reduce_fusion
  159.6 1.3 fusion.37
  160.9 9.8 %custom-call.7 = f32[1,128,128]{1,2,0:T(8,128)S(1)} custom-call(f32[1,128,128]{2,1,0:T(8,128)S(1)} %get-tuple-element.18), custom_call_target="InvertDiagBlocksLowerTriangular" | custom-call | tf_op jit(solution)/shard_map/jit(_solve_triangular)/triangular_solve | solution.py:71
  170.7 2.7 %convolution_multiply_fusion = f32[128,4384]{0,1:T(8,128)} fusion(bf16[128,4384]{1,0:T(8,128)(2,1)S(1)} %bitcast.99, f32[1,128,128]{1,2,0:T(8,128)S(1)} %custom-call.7), kind=kOutput, calls=%fused_computation.2 | convolution fusion | flops 862490624 | bytes 3432448 | tf_op jit(solution)/shard_map/jit(_solve_triangular)/triangular_solve | solution.py:71
  (4 shorter events, 0.1 us)
Async XLA Ops:
  0.6 79.9 %collective-permute-start = (bf16[64,8768]{1,0:T(8,128)(2,1)}, bf16[64,8768]{1,0:T(8,128)(2,1)S(1)}, u32[]{:S(2)}, u32[]{:S(2)}) collective-permute-start(bf16[64,8768]{1,0:T(8,128)(2,1)} %param.2), channel_id=1, source_target_pairs={} | collective-permute-start | bytes 3366920 | tf_op jit(solution)/shard_map/ppermute | solution.py:10
  1.4 79.1 %collective-permute-start.1 = (bf16[64,8768]{1,0:T(8,128)(2,1)}, bf16[64,8768]{1,0:T(8,128)(2,1)}, u32[]{:S(2)}, u32[]{:S(2)}) collective-permute-start(bf16[64,8768]{1,0:T(8,128)(2,1)} %param.2), channel_id=1, source_target_pairs={{0,1},{2,3},{4,5},{6,7},{8,9},{10,11},{12,13},{14,15},{16,17},{18,... | collective-permute-start | bytes 3366920 | tf_op jit(solution)/shard_map/ppermute | solution.py:10
  8.2 72.3 %copy-start = (bf16[64,8768]{1,0:T(8,128)(2,1)S(1)}, bf16[64,8768]{1,0:T(8,128)(2,1)}, u32[]{:S(2)}) copy-start(bf16[64,8768]{1,0:T(8,128)(2,1)} %param.2) | copy-start | bytes 3366916
where the time goes:
time: 174 us; the launch traced here: 173 us
  local copies, waits for them, and re-layouts  74.4 us (43%)
  blocking collectives  60 us (34%)
  other arithmetic  24.7 us (14%)
  matrix products  6.89 us (4%)
  starting transfers between devices  6.63 us (4%)
    gather x2, local copies, waits for them, and re-layouts, banded_matrix(): coefficients[safe]  72.3 us
    psum x1, blocking collectives, summed_gram(): stacked = lax.psum(jnp.stack(listing), ('space', 'tm'))  42.9 us
    all_to_all x1, blocking collectives, body(): lax.all_to_all(outgoing, 'tm', split_axis=1, concat_axis=0, tiled=True)  17.1 us
    another operation x3, other arithmetic, body(): lower_one = jnp.linalg.cholesky(gram)  12.4 us
    another operation x1, other arithmetic, body(): jax.scipy.linalg.solve_triangular(lower_one, arrived.astype(jnp.float32),...  9.81 us
    ppermute x2, starting transfers between devices, shifted(): return lax.ppermute(block, axis, route)  6.63 us
  transfers between devices with their start and end apart: 2, of which 0 were waited for; matrix products, arithmetic and copies ran while one was open for 42% of the time, Pallas kernels for 0%

commit v1 on v0

v1 whole, which is shorter than its diff:
```python
import functools
import math

import jax
import jax.numpy as jnp
from jax import lax
from jax.experimental import pallas as pl
from jax.experimental.pallas import tpu as pltpu
from jax.sharding import PartitionSpec as P

LANES = 128
SUB = 8
PLANE = 4
CHUNKS = 5
MESH = pl.DeviceIdType.MESH


def banded(coefficients, rows, cols, delay):
    lag = (
        lax.broadcasted_iota(jnp.int32, (rows, cols), 0)
        + delay
        - lax.broadcasted_iota(jnp.int32, (rows, cols), 1)
    )
    one_hot = lag[:, :, None] == lax.broadcasted_iota(
        jnp.int32, (1, 1, coefficients.shape[0]), 2
    )
    return jnp.sum(jnp.where(one_hot, coefficients.astype(jnp.float32), 0.0), axis=2).astype(
        coefficients.dtype
    )


def general_body(thermal_anomaly, smoothing_coefs):
    steps = thermal_anomaly.shape[0]
    blocks = lax.axis_size("tm")
    coefficients = jnp.concatenate([jnp.ones((1,), jnp.float32), smoothing_coefs]).astype(
        jnp.bfloat16
    )
    reach = min(blocks - 1, -(-(coefficients.shape[0] - 1) // steps))
    record = [thermal_anomaly]
    for distance in range(1, reach + 1):
        route = [(i, i + distance) for i in range(blocks - distance)]
        record.insert(0, lax.ppermute(thermal_anomaly, "tm", route))
    matrix = banded(coefficients, steps, (reach + 1) * steps, reach * steps)
    outgoing = jnp.dot(
        matrix, jnp.concatenate(record, axis=0), preferred_element_type=jnp.float32
    ).astype(jnp.bfloat16)
    arrived = lax.all_to_all(outgoing, "tm", split_axis=1, concat_axis=0, tiled=True)
    gram = lax.psum(
        jnp.dot(arrived, arrived.T, preferred_element_type=jnp.float32), ("space", "tm")
    )
    lower = jnp.linalg.cholesky(gram)
    rows = jax.scipy.linalg.solve_triangular(lower, arrived.astype(jnp.float32), lower=True)
    scale = jnp.sqrt(jnp.float32(thermal_anomaly.shape[1] * lax.axis_size("space")))
    return rows * scale, lower / scale


def place(dst, rows, x_ref, base, start, width, half):
    valid = min(width, half - start)
    low = base + start
    aligned = low // LANES * LANES
    shift = low - aligned
    end = min(aligned + pl.cdiv(shift + valid, LANES) * LANES, x_ref.shape[1])
    value = x_ref[:, aligned:end][:, shift : shift + valid]
    if valid < width:
        edge = valid // LANES * LANES
        dst[rows, start + edge : start + width] = jnp.zeros(
            (value.shape[0], width - edge), dst.dtype
        )
    dst[rows, start : start + valid] = value


def gather_kernel(
    spans,
    x_ref,
    coef_ref,
    filtered_ref,
    gram_ref,
    outgoing,
    panel,
    partial,
    pieces,
    reduced,
    planes,
    whole,
    swap_send,
    swap_recv,
    rs_send,
    rs_recv,
    line_send,
    line_recv,
    ag_send,
    ag_recv,
):
    space = lax.axis_index("space")
    tm = lax.axis_index("tm")
    inner = space % PLANE
    plane = space // PLANE
    lines = lax.axis_size("space") // PLANE
    group = PLANE * 2
    me = inner * 2 + tm
    hours = x_ref.shape[0]
    total = 2 * hours
    half = x_ref.shape[1] // 2
    share = total // group

    def in_group(offset):
        other = (me + offset) % group
        return other, (plane * PLANE + other // 2, other % 2)

    def in_line(offset):
        return ((plane + offset) % lines * PLANE + inner, tm)

    barrier = pltpu.get_barrier_semaphore()
    for offset in range(1, group):
        pl.semaphore_signal(barrier, inc=1, device_id=in_group(offset)[1], device_id_type=MESH)
    for offset in range(1, lines):
        pl.semaphore_signal(barrier, inc=1, device_id=in_line(offset), device_id_type=MESH)

    for side in range(2):

        @pl.when(tm == side)
        def _():
            for start, width in spans:
                place(outgoing, slice(None), x_ref, (1 - side) * half, start, width, half)

    pl.semaphore_wait(barrier, group - 1 + lines - 1)

    swaps = []
    for index, (start, width) in enumerate(spans):
        copy = pltpu.make_async_remote_copy(
            src_ref=outgoing.at[:, pl.ds(start, width)],
            dst_ref=panel.at[pl.ds(pl.multiple_of(tm * hours, hours), hours), pl.ds(start, width)],
            send_sem=swap_send.at[index],
            recv_sem=swap_recv.at[index],
            device_id=(space, 1 - tm),
            device_id_type=MESH,
        )
        copy.start()
        swaps.append(copy)

    for side in range(2):

        @pl.when(tm == side)
        def _():
            rows = slice(side * hours, (side + 1) * hours)
            for start, width in spans:
                place(panel, rows, x_ref, side * half, start, width, half)

    row = lax.broadcasted_iota(jnp.int32, (total, total), 0)
    col = lax.broadcasted_iota(jnp.int32, (total, total), 1)
    lagged = jnp.broadcast_to(coef_ref[...], (total, total))
    lagged = pltpu.roll(lagged, 1, axis=1, stride=1, stride_axis=0)
    turned = jnp.where(col > row, lagged, jnp.where(col == row, 1.0, 0.0))
    matrix = turned.T.astype(jnp.bfloat16)

    partial[...] = jnp.zeros_like(partial)
    for index, (start, width) in enumerate(spans):
        swaps[index].wait_recv()
        values = jnp.dot(
            matrix, panel[:, start : start + width], preferred_element_type=jnp.float32
        ).astype(jnp.bfloat16)
        filtered_ref[:, start : start + width] = values
        partial[...] += lax.dot_general(
            values, values, (((1,), (1,)), ((), ())), preferred_element_type=jnp.float32
        )

    copies = []
    for offset in range(1, group):
        other, device = in_group(offset)
        copy = pltpu.make_async_remote_copy(
            src_ref=partial.at[pl.ds(pl.multiple_of(other * share, share), share)],
            dst_ref=pieces.at[offset - 1],
            send_sem=rs_send.at[offset - 1],
            recv_sem=rs_recv.at[offset - 1],
            device_id=device,
            device_id_type=MESH,
        )
        copy.start()
        copies.append(copy)
    mine = pl.ds(pl.multiple_of(me * share, share), share)
    running = partial[mine, :]
    for offset in range(1, group):
        copies[offset - 1].wait_recv()
        running = running + pieces[offset - 1]
    reduced[...] = running
    planes[plane] = running

    for offset in range(1, lines):
        copy = pltpu.make_async_remote_copy(
            src_ref=reduced,
            dst_ref=planes.at[plane],
            send_sem=line_send.at[offset - 1],
            recv_sem=line_recv.at[offset - 1],
            device_id=in_line(offset),
            device_id_type=MESH,
        )
        copy.start()
        copies.append(copy)
    for offset in range(1, lines):
        copies[group - 1 + offset - 1].wait_recv()
    running = planes[0]
    for index in range(1, lines):
        running = running + planes[index]
    whole[mine, :] = running

    for offset in range(1, group):
        copy = pltpu.make_async_remote_copy(
            src_ref=whole.at[mine],
            dst_ref=whole.at[mine],
            send_sem=ag_send.at[offset - 1],
            recv_sem=ag_recv.at[offset - 1],
            device_id=in_group(offset)[1],
            device_id_type=MESH,
        )
        copy.start()
        copies.append(copy)
    for copy in copies[-(group - 1) :]:
        copy.wait_recv()
    gram_ref[...] = whole[...]
    for copy in swaps + copies:
        copy.wait_send()


def factor(gram_ref, points):
    size = gram_ref.shape[0]
    count = size // SUB
    blocks = [gram_ref[SUB * b : SUB * (b + 1), :] for b in range(count)]
    lane = lax.broadcasted_iota(jnp.int32, (SUB, size), 1)
    sub = lax.broadcasted_iota(jnp.int32, (SUB, size), 0)
    pivots = [jnp.zeros((SUB, size), jnp.float32) for _ in range(count)]
    for k in range(size):
        b, r = divmod(k, SUB)
        columns = [
            jnp.broadcast_to(blocks[i][:, k : k + 1], (SUB, size)) for i in range(b, count)
        ]
        pivot = jnp.broadcast_to(columns[0][r : r + 1, :], (SUB, size))
        row = jnp.broadcast_to(blocks[b][r : r + 1, :], (SUB, size))
        pivots[b] = jnp.where(sub == r, pivot, pivots[b])
        here = lane == k
        ratio = jnp.where(here, 1.0, row) / pivot
        for i in range(b, count):
            new = jnp.where(here, 0.0, blocks[i]) - columns[i - b] * ratio
            blocks[i] = jnp.where(sub > r, new, blocks[i]) if i == b else new
    return blocks, pivots


def basis_kernel(points, gram_ref, filtered_ref, basis_ref, factor_ref, high, low, upper):
    @pl.when(pl.program_id(0) == 0)
    def _():
        size = gram_ref.shape[0]
        blocks, pivots = factor(gram_ref, points)
        lane = lax.broadcasted_iota(jnp.int32, (SUB, size), 1)
        sub = lax.broadcasted_iota(jnp.int32, (SUB, size), 0)
        root = math.sqrt(points)
        for b, (block, pivot) in enumerate(zip(blocks, pivots)):
            diagonal = jnp.sqrt(pivot)
            here = lane == sub + b * SUB
            below = lane < sub + b * SUB
            inverse = jnp.where(here, 1.0, jnp.where(below, block, 0.0)) * (root / diagonal)
            rows = slice(b * SUB, (b + 1) * SUB)
            top = inverse.astype(jnp.bfloat16).astype(jnp.float32)
            high[rows, :] = top
            low[rows, :] = inverse - top
            upper[rows, :] = jnp.where(here, pivot, jnp.where(below, 0.0, block)) / (
                diagonal * root
            )
        factor_ref[...] = upper[...].T

    values = filtered_ref[...]
    basis_ref[...] = jnp.dot(
        high[...].astype(jnp.bfloat16), values, preferred_element_type=jnp.float32
    ) + jnp.dot(low[...].astype(jnp.bfloat16), values, preferred_element_type=jnp.float32)


def paired_body(thermal_anomaly, smoothing_coefs):
    hours, sites = thermal_anomaly.shape
    total = 2 * hours
    half = sites // 2
    tiles = pl.cdiv(half, LANES)
    step = pl.cdiv(tiles, CHUNKS)
    spans = [
        (t * LANES, min(step, tiles - t) * LANES) for t in range(0, tiles, step)
    ]
    padded = tiles * LANES
    group = PLANE * 2
    lines = lax.axis_size("space") // PLANE
    share = total // group
    dma = pltpu.SemaphoreType.DMA
    vmem = pl.BlockSpec(memory_space=pltpu.VMEM)
    filtered, gram = pl.pallas_call(
        functools.partial(gather_kernel, spans),
        out_shape=(
            jax.ShapeDtypeStruct((total, padded), jnp.bfloat16),
            jax.ShapeDtypeStruct((total, total), jnp.float32),
        ),
        in_specs=[vmem, vmem],
        out_specs=(vmem, vmem),
        scratch_shapes=[
            pltpu.VMEM((hours, padded), jnp.bfloat16),
            pltpu.VMEM((total, padded), jnp.bfloat16),
            pltpu.VMEM((total, total), jnp.float32),
            pltpu.VMEM((group - 1, share, total), jnp.float32),
            pltpu.VMEM((share, total), jnp.float32),
            pltpu.VMEM((lines, share, total), jnp.float32),
            pltpu.VMEM((total, total), jnp.float32),
            dma((len(spans),)),
            dma((len(spans),)),
            dma((group - 1,)),
            dma((group - 1,)),
            dma((lines - 1,)),
            dma((lines - 1,)),
            dma((group - 1,)),
            dma((group - 1,)),
        ],
        compiler_params=pltpu.CompilerParams(collective_id=0, has_side_effects=True),
        name="gather_gram",
    )(thermal_anomaly, smoothing_coefs[: total].reshape(1, total))

    width = step * LANES
    points = sites * lax.axis_size("space")
    return pl.pallas_call(
        functools.partial(basis_kernel, points),
        grid=(pl.cdiv(half, width),),
        out_shape=(
            jax.ShapeDtypeStruct((total, half), jnp.float32),
            jax.ShapeDtypeStruct((total, total), jnp.float32),
        ),
        in_specs=[
            pl.BlockSpec((total, total), lambda i: (0, 0)),
            pl.BlockSpec((total, width), lambda i: (0, i)),
        ],
        out_specs=(
            pl.BlockSpec((total, width), lambda i: (0, i)),
            pl.BlockSpec((total, total), lambda i: (0, 0)),
        ),
        scratch_shapes=[pltpu.VMEM((total, total), jnp.float32)] * 3,
        name="factor_basis",
    )(gram, filtered)


def body(thermal_anomaly, smoothing_coefs):
    hours, sites = thermal_anomaly.shape
    paired = (
        lax.axis_size("tm") == 2
        and 2 * hours == LANES
        and smoothing_coefs.shape[0] >= LANES
        and sites % 2 == 0
        and lax.axis_size("space") % PLANE == 0
        and lax.axis_size("space") > PLANE
    )
    return (paired_body if paired else general_body)(thermal_anomaly, smoothing_coefs)


def solution(mesh):
    placed = (P("tm", "space"), P())
    return jax.shard_map(
        body, mesh=mesh, in_specs=placed, out_specs=(P(None, ("space", "tm")), P()), check_vma=False
    )
```

time: 174 us -> 58.5 us (0.34)
  local copies, waits for them, and re-layouts: 74.4 us -> 3.01 us
  blocking collectives: 60 us -> 0 us
  Pallas kernels: 0 us -> 54.6 us
  other arithmetic: 24.7 us -> 0 us
  matrix products: 6.89 us -> 0 us
  starting transfers between devices: 6.63 us -> 0 us
    gather x2 -> x0, local copies, waits for them, and re-layouts: 72.3 us -> none  [banded_matrix(): coefficients[safe]]
    pallas_call x0 -> x2, Pallas kernels: none -> 54.6 us  [the longest x1 32.4 us: paired_body(): pl.pallas_call(functools.partial(gather_kernel, spans), out_shape=(jax.Sh...]
    psum x1 -> x0, blocking collectives: 42.9 us -> none  [summed_gram(): stacked = lax.psum(jnp.stack(listing), ('space', 'tm'))]
    another operation x5 -> x0, other arithmetic: 22.9 us -> none  [the longest x3 12.4 us: body(): lower_one = jnp.linalg.cholesky(gram)]
    all_to_all x1 -> x0, blocking collectives: 17.1 us -> none  [body(): lax.all_to_all(outgoing, 'tm', split_axis=1, concat_axis=0, tiled=True)]
    ppermute x2 -> x0, starting transfers between devices: 6.63 us -> none  [shifted(): return lax.ppermute(block, axis, route)]
    dot_general x11 -> x0, matrix products: 4.19 us -> none  [the longest x10 2.12 us: product_low(): return jnp.dot(left, right.T, preferred_element_type=jnp.float32)]
    pallas_call x0 -> x1, local copies, waits for them, and re-layouts: none -> 3.01 us  [paired_body(): pl.pallas_call(functools.partial(basis_kernel, points), grid=(pl.cdiv(hal...]
  transfers between devices with their start and end apart: 2 -> 0, of which waited for: 0 -> 0; matrix products, arithmetic and copies ran while one was open for 42% -> 0% of each run, Pallas kernels for 0% -> 0%
where the time goes in v1:
time: 58.5 us; the launch traced here: 58.2 us
  Pallas kernels  54.6 us (93%)
  local copies, waits for them, and re-layouts  3.01 us (5%)
  between operations  0.64 us (1%)
    pallas_call x1, Pallas kernels, paired_body(): pl.pallas_call(functools.partial(gather_kernel, spans), out_shape=(jax.Sh...  32.4 us
    pallas_call x1, Pallas kernels, paired_body(): pl.pallas_call(functools.partial(basis_kernel, points), grid=(pl.cdiv(hal...  22.2 us
    pallas_call x1, local copies, waits for them, and re-layouts, paired_body(): pl.pallas_call(functools.partial(basis_kernel, points), grid=(pl.cdiv(hal...  3.01 us

profile of v1, /device:TPU:0, one launch (start us, length us, event | category | flops | bytes accessed | tf_op | source)
XLA Modules:
  0.0 58.2 jit_solution(11321408607043298185)
XLA Ops:
  0.6 32.4 %gather_gram.1 = (bf16[128,4480]{1,0:T(8,128)(2,1)}, f32[128,128]{1,0:T(8,128)}) custom-call(bf16[64,8768]{1,0:T(8,128)(2,1)} %x_ref.1, f32[1,128]{1,0:T(1,128)} %bitcast.1), custom_call_target="tpu_custom_call" | custom-call | tf_op jit(solution)/shard_map/gather_gram/pallas_call | solution.py:290
  33.0 22.2 %factor_basis.1 = (f32[128,4384]{1,0:T(8,128)}, f32[128,128]{1,0:T(8,128)}) custom-call(f32[128,128]{1,0:T(8,128)} %get-tuple-element.4.gram_ref, bf16[128,4480]{1,0:T(8,128)(2,1)} %get-tuple-element.5.filtered_ref), custom_call_target="tpu_custom_call" | custom-call | tf_op jit(solution)/shard_map/factor_basis/pallas_call | solution.py:321
  55.2 3.0 %copy.4 = f32[128,4384]{0,1:T(8,128)} copy(f32[128,4384]{1,0:T(8,128)} %get-tuple-element.6) | data formatting | bytes 4489216 | tf_op jit(solution)/shard_map/factor_basis/pallas_call | solution.py:321

commit v2 on v1

--- a/solution.py
+++ b/solution.py
@@ -159,7 +159,7 @@
         values = jnp.dot(
             matrix, panel[:, start : start + width], preferred_element_type=jnp.float32
         ).astype(jnp.bfloat16)
-        filtered_ref[:, start : start + width] = values
+        filtered_ref[start : start + width, :] = values.T
         partial[...] += lax.dot_general(
             values, values, (((1,), (1,)), ((), ())), preferred_element_type=jnp.float32
         )
@@ -221,55 +221,91 @@
         copy.wait_send()
 
 
-def factor(gram_ref, points):
+def factor(gram_ref, store):
     size = gram_ref.shape[0]
     count = size // SUB
+    full = (SUB, size)
     blocks = [gram_ref[SUB * b : SUB * (b + 1), :] for b in range(count)]
-    lane = lax.broadcasted_iota(jnp.int32, (SUB, size), 1)
-    sub = lax.broadcasted_iota(jnp.int32, (SUB, size), 0)
-    pivots = [jnp.zeros((SUB, size), jnp.float32) for _ in range(count)]
-    for k in range(size):
-        b, r = divmod(k, SUB)
+    lane = lax.broadcasted_iota(jnp.int32, full, 1)
+    sub = lax.broadcasted_iota(jnp.int32, full, 0)
+    for b in range(count):
+        first = b * SUB
+        inside = (lane >= first) & (lane < first + SUB)
         columns = [
-            jnp.broadcast_to(blocks[i][:, k : k + 1], (SUB, size)) for i in range(b, count)
+            [jnp.broadcast_to(blocks[i][:, first + c : first + c + 1], full) for c in range(SUB)]
+            for i in range(b, count)
         ]
-        pivot = jnp.broadcast_to(columns[0][r : r + 1, :], (SUB, size))
-        row = jnp.broadcast_to(blocks[b][r : r + 1, :], (SUB, size))
-        pivots[b] = jnp.where(sub == r, pivot, pivots[b])
-        here = lane == k
-        ratio = jnp.where(here, 1.0, row) / pivot
-        for i in range(b, count):
-            new = jnp.where(here, 0.0, blocks[i]) - columns[i - b] * ratio
-            blocks[i] = jnp.where(sub > r, new, blocks[i]) if i == b else new
-    return blocks, pivots
-
-
-def basis_kernel(points, gram_ref, filtered_ref, basis_ref, factor_ref, high, low, upper):
+        upper = [
+            [
+                jnp.broadcast_to(columns[0][c][r : r + 1, :], full) if c >= r else None
+                for c in range(SUB)
+            ]
+            for r in range(SUB)
+        ]
+        rows = [
+            jnp.where(
+                inside,
+                jnp.where(lane == first + r, 1.0, 0.0),
+                jnp.broadcast_to(blocks[b][r : r + 1, :], full),
+            )
+            for r in range(SUB)
+        ]
+        unit = [[None] * SUB for _ in range(SUB)]
+        inverse = [None] * SUB
+        for c in range(SUB):
+            inverse[c] = 1.0 / upper[c][c]
+            for r in range(c + 1, SUB):
+                unit[c][r] = upper[c][r] * inverse[c]
+                for j in range(r, SUB):
+                    upper[r][j] = upper[r][j] - unit[c][r] * upper[c][j]
+                rows[r] = rows[r] - unit[c][r] * rows[c]
+        store(b, rows, upper, lane, sub)
+        solved = [rows[r] * inverse[r] for r in range(SUB)]
+        for c in range(SUB - 1, 0, -1):
+            for r in range(c):
+                solved[r] = solved[r] - unit[r][c] * solved[c]
+        for i in range(b + 1, count):
+            terms = [columns[i - b][c] * solved[c] for c in range(SUB)]
+            while len(terms) > 1:
+                terms = [terms[t] + terms[t + 1] for t in range(0, len(terms), 2)]
+            blocks[i] = jnp.where(inside, 0.0, blocks[i]) - terms[0]
+
+
+def basis_kernel(points, gram_ref, filtered_ref, basis_ref, factor_ref, split, turned):
+    size = gram_ref.shape[0]
+    root = math.sqrt(points)
+
+    def store(b, rows, upper, lane, sub):
+        first = b * SUB
+        block = rows[0]
+        pivot = upper[0][0]
+        for r in range(1, SUB):
+            block = jnp.where(sub == r, rows[r], block)
+            pivot = jnp.where(sub == r, upper[r][r], pivot)
+        corner = block
+        for r in range(SUB):
+            for c in range(r, SUB):
+                corner = jnp.where((sub == r) & (lane == first + c), upper[r][c], corner)
+        diagonal = jnp.sqrt(pivot)
+        here = slice(first, first + SUB)
+        inverse = jnp.where(lane <= sub + first, block, 0.0) * (root / diagonal)
+        top = inverse.astype(jnp.bfloat16).astype(jnp.float32)
+        split[here, :] = top
+        split[size + first : size + first + SUB, :] = inverse - top
+        turned[here, :] = jnp.where(lane >= sub + first, corner, 0.0) / (diagonal * root)
+
     @pl.when(pl.program_id(0) == 0)
     def _():
-        size = gram_ref.shape[0]
-        blocks, pivots = factor(gram_ref, points)
-        lane = lax.broadcasted_iota(jnp.int32, (SUB, size), 1)
-        sub = lax.broadcasted_iota(jnp.int32, (SUB, size), 0)
-        root = math.sqrt(points)
-        for b, (block, pivot) in enumerate(zip(blocks, pivots)):
-            diagonal = jnp.sqrt(pivot)
-            here = lane == sub + b * SUB
-            below = lane < sub + b * SUB
-            inverse = jnp.where(here, 1.0, jnp.where(below, block, 0.0)) * (root / diagonal)
-            rows = slice(b * SUB, (b + 1) * SUB)
-            top = inverse.astype(jnp.bfloat16).astype(jnp.float32)
-            high[rows, :] = top
-            low[rows, :] = inverse - top
-            upper[rows, :] = jnp.where(here, pivot, jnp.where(below, 0.0, block)) / (
-                diagonal * root
-            )
-        factor_ref[...] = upper[...].T
-
-    values = filtered_ref[...]
-    basis_ref[...] = jnp.dot(
-        high[...].astype(jnp.bfloat16), values, preferred_element_type=jnp.float32
-    ) + jnp.dot(low[...].astype(jnp.bfloat16), values, preferred_element_type=jnp.float32)
+        factor(gram_ref, store)
+        factor_ref[...] = turned[...].T
+
+    both = lax.dot_general(
+        filtered_ref[...],
+        split[...].astype(jnp.bfloat16),
+        (((1,), (1,)), ((), ())),
+        preferred_element_type=jnp.float32,
+    )
+    basis_ref[...] = both[:, :size] + both[:, size:]
 
 
 def paired_body(thermal_anomaly, smoothing_coefs):
@@ -290,7 +326,7 @@
     filtered, gram = pl.pallas_call(
         functools.partial(gather_kernel, spans),
         out_shape=(
-            jax.ShapeDtypeStruct((total, padded), jnp.bfloat16),
+            jax.ShapeDtypeStruct((padded, total), jnp.bfloat16),
             jax.ShapeDtypeStruct((total, total), jnp.float32),
         ),
         in_specs=[vmem, vmem],
@@ -318,24 +354,28 @@
 
     width = step * LANES
     points = sites * lax.axis_size("space")
-    return pl.pallas_call(
+    basis, lower = pl.pallas_call(
         functools.partial(basis_kernel, points),
         grid=(pl.cdiv(half, width),),
         out_shape=(
-            jax.ShapeDtypeStruct((total, half), jnp.float32),
+            jax.ShapeDtypeStruct((half, total), jnp.float32),
             jax.ShapeDtypeStruct((total, total), jnp.float32),
         ),
         in_specs=[
             pl.BlockSpec((total, total), lambda i: (0, 0)),
-            pl.BlockSpec((total, width), lambda i: (0, i)),
+            pl.BlockSpec((width, total), lambda i: (i, 0)),
         ],
         out_specs=(
-            pl.BlockSpec((total, width), lambda i: (0, i)),
+            pl.BlockSpec((width, total), lambda i: (i, 0)),
             pl.BlockSpec((total, total), lambda i: (0, 0)),
         ),
-        scratch_shapes=[pltpu.VMEM((total, total), jnp.float32)] * 3,
+        scratch_shapes=[
+            pltpu.VMEM((2 * total, total), jnp.float32),
+            pltpu.VMEM((total, total), jnp.float32),
+        ],
         name="factor_basis",
     )(gram, filtered)
+    return basis.T, lower
 
 
 def body(thermal_anomaly, smoothing_coefs):

time: 58.5 us -> 43 us (0.74)
  Pallas kernels: 54.6 us -> 42.1 us
  local copies, waits for them, and re-layouts: 3.01 us -> 0 us
    pallas_call x1, Pallas kernels: 22.2 us -> 9.75 us  [paired_body(): pl.pallas_call(functools.partial(basis_kernel, points), grid=(pl.cdiv(hal...]
    pallas_call x1 -> x0, local copies, waits for them, and re-layouts: 3.01 us -> none  [paired_body(): pl.pallas_call(functools.partial(basis_kernel, points), grid=(pl.cdiv(hal...]
where the time goes in v2:
time: 43 us; the launch traced here: 42.8 us
  Pallas kernels  42.1 us (98%)
  between operations  0.64 us (1%)
    pallas_call x1, Pallas kernels, paired_body(): pl.pallas_call(functools.partial(gather_kernel, spans), out_shape=(jax.Sh...  32.4 us
    pallas_call x1, Pallas kernels, paired_body(): pl.pallas_call(functools.partial(basis_kernel, points), grid=(pl.cdiv(hal...  9.75 us

profile of v2, /device:TPU:0, one launch (start us, length us, event | category | flops | bytes accessed | tf_op | source)
XLA Modules:
  0.0 42.8 jit_solution(11968328415824177799)
XLA Ops:
  0.6 32.4 %gather_gram.1 = (bf16[4480,128]{1,0:T(8,128)(2,1)}, f32[128,128]{1,0:T(8,128)}) custom-call(bf16[64,8768]{1,0:T(8,128)(2,1)} %x_ref.1, f32[1,128]{1,0:T(1,128)} %bitcast.2), custom_call_target="tpu_custom_call" | custom-call | tf_op jit(solution)/shard_map/gather_gram/pallas_call | solution.py:326
  33.0 9.7 %factor_basis.1 = (f32[4384,128]{1,0:T(8,128)}, f32[128,128]{1,0:T(8,128)}) custom-call(f32[128,128]{1,0:T(8,128)} %get-tuple-element.6.gram_ref, bf16[4480,128]{1,0:T(8,128)(2,1)} %get-tuple-element.7.filtered_ref), custom_call_target="tpu_custom_call" | custom-call | tf_op jit(solution)/shard_map/factor_basis/pallas_call | solution.py:357

commit v3 on v2

--- a/solution.py
+++ b/solution.py
@@ -12,6 +12,7 @@
 SUB = 8
 PLANE = 4
 CHUNKS = 5
+SLABS = 4
 MESH = pl.DeviceIdType.MESH
 
 
@@ -71,10 +72,15 @@
 
 def gather_kernel(
     spans,
+    x_hbm,
+    coef_hbm,
+    filtered_hbm,
+    gram_ref,
     x_ref,
     coef_ref,
     filtered_ref,
-    gram_ref,
+    load_sem,
+    store_sem,
     outgoing,
     panel,
     partial,
@@ -116,17 +122,30 @@
     for offset in range(1, lines):
         pl.semaphore_signal(barrier, inc=1, device_id=in_line(offset), device_id_type=MESH)
 
-    for side in range(2):
-
-        @pl.when(tm == side)
-        def _():
-            for start, width in spans:
-                place(outgoing, slice(None), x_ref, (1 - side) * half, start, width, half)
-
-    pl.semaphore_wait(barrier, group - 1 + lines - 1)
+    slab = hours // SLABS
+    loads = [
+        pltpu.make_async_copy(
+            x_hbm.at[pl.ds(slab * index, slab)],
+            x_ref.at[pl.ds(slab * index, slab)],
+            load_sem.at[index],
+        )
+        for index in range(SLABS)
+    ] + [pltpu.make_async_copy(coef_hbm, coef_ref, load_sem.at[SLABS])]
+    for copy in loads:
+        copy.start()
+    for copy in loads:
+        copy.wait()
 
     swaps = []
     for index, (start, width) in enumerate(spans):
+        for side in range(2):
+
+            @pl.when(tm == side)
+            def _():
+                place(outgoing, slice(None), x_ref, (1 - side) * half, start, width, half)
+
+        if index == 0:
+            pl.semaphore_wait(barrier, group - 1 + lines - 1)
         copy = pltpu.make_async_remote_copy(
             src_ref=outgoing.at[:, pl.ds(start, width)],
             dst_ref=panel.at[pl.ds(pl.multiple_of(tm * hours, hours), hours), pl.ds(start, width)],
@@ -153,6 +172,7 @@
     turned = jnp.where(col > row, lagged, jnp.where(col == row, 1.0, 0.0))
     matrix = turned.T.astype(jnp.bfloat16)
 
+    stores = []
     partial[...] = jnp.zeros_like(partial)
     for index, (start, width) in enumerate(spans):
         swaps[index].wait_recv()
@@ -160,6 +180,13 @@
             matrix, panel[:, start : start + width], preferred_element_type=jnp.float32
         ).astype(jnp.bfloat16)
         filtered_ref[start : start + width, :] = values.T
+        store = pltpu.make_async_copy(
+            filtered_ref.at[pl.ds(start, width)],
+            filtered_hbm.at[pl.ds(start, width)],
+            store_sem.at[index],
+        )
+        store.start()
+        stores.append(store)
         partial[...] += lax.dot_general(
             values, values, (((1,), (1,)), ((), ())), preferred_element_type=jnp.float32
         )
@@ -219,6 +246,8 @@
     gram_ref[...] = whole[...]
     for copy in swaps + copies:
         copy.wait_send()
+    for store in stores:
+        store.wait()
 
 
 def factor(gram_ref, store):
@@ -323,15 +352,21 @@
     share = total // group
     dma = pltpu.SemaphoreType.DMA
     vmem = pl.BlockSpec(memory_space=pltpu.VMEM)
+    anywhere = pl.BlockSpec(memory_space=pl.ANY)
     filtered, gram = pl.pallas_call(
         functools.partial(gather_kernel, spans),
         out_shape=(
             jax.ShapeDtypeStruct((padded, total), jnp.bfloat16),
             jax.ShapeDtypeStruct((total, total), jnp.float32),
         ),
-        in_specs=[vmem, vmem],
-        out_specs=(vmem, vmem),
+        in_specs=[anywhere, anywhere],
+        out_specs=(anywhere, vmem),
         scratch_shapes=[
+            pltpu.VMEM((hours, sites), jnp.bfloat16),
+            pltpu.VMEM((1, total), jnp.float32),
+            pltpu.VMEM((padded, total), jnp.bfloat16),
+            dma((SLABS + 1,)),
+            dma((len(spans),)),
             pltpu.VMEM((hours, padded), jnp.bfloat16),
             pltpu.VMEM((total, padded), jnp.bfloat16),
             pltpu.VMEM((total, total), jnp.float32),

time: 43 us -> 41.6 us (0.967)
  Pallas kernels: 42.1 us -> 40.7 us
    pallas_call x1, Pallas kernels: 32.4 us -> 31 us  [paired_body(): pl.pallas_call(functools.partial(gather_kernel, spans), out_shape=(jax.Sh...]
where the time goes in v3:
time: 41.6 us; the launch traced here: 41.3 us
  Pallas kernels  40.7 us (98%)
  between operations  0.64 us (2%)
    pallas_call x1, Pallas kernels, paired_body(): pl.pallas_call(functools.partial(gather_kernel, spans), out_shape=(jax.Sh...  31 us
    pallas_call x1, Pallas kernels, paired_body(): pl.pallas_call(functools.partial(basis_kernel, points), grid=(pl.cdiv(hal...  9.75 us

profile of v3, /device:TPU:0, one launch (start us, length us, event | category | flops | bytes accessed | tf_op | source)
XLA Modules:
  0.0 41.3 jit_solution(12001560825538548317)
XLA Ops:
  0.6 31.0 %gather_gram.1 = (bf16[4480,128]{1,0:T(8,128)(2,1)}, f32[128,128]{1,0:T(8,128)}) custom-call(bf16[64,8768]{1,0:T(8,128)(2,1)} %x_hbm.1, f32[1,128]{1,0:T(1,128)} %bitcast.2), custom_call_target="tpu_custom_call" | custom-call | tf_op jit(solution)/shard_map/gather_gram/pallas_call | solution.py:356
  31.6 9.7 %factor_basis.1 = (f32[4384,128]{1,0:T(8,128)}, f32[128,128]{1,0:T(8,128)}) custom-call(f32[128,128]{1,0:T(8,128)} %get-tuple-element.6.gram_ref, bf16[4480,128]{1,0:T(8,128)(2,1)} %get-tuple-element.7.filtered_ref), custom_call_target="tpu_custom_call" | custom-call | tf_op jit(solution)/shard_map/factor_basis/pallas_call | solution.py:392

commit v4 on v3

--- a/solution.py
+++ b/solution.py
@@ -300,8 +300,24 @@
             blocks[i] = jnp.where(inside, 0.0, blocks[i]) - terms[0]
 
 
-def basis_kernel(points, gram_ref, filtered_ref, basis_ref, factor_ref, split, turned):
+def basis_kernel(
+    points,
+    spans,
+    gram_ref,
+    filtered_hbm,
+    basis_hbm,
+    factor_hbm,
+    filtered_ref,
+    basis_ref,
+    factor_ref,
+    split,
+    turned,
+    load_sem,
+    store_sem,
+):
     size = gram_ref.shape[0]
+    load = pltpu.make_async_copy(filtered_hbm, filtered_ref, load_sem)
+    load.start()
     root = math.sqrt(points)
 
     def store(b, rows, upper, lane, sub):
@@ -323,18 +339,31 @@
         split[size + first : size + first + SUB, :] = inverse - top
         turned[here, :] = jnp.where(lane >= sub + first, corner, 0.0) / (diagonal * root)
 
-    @pl.when(pl.program_id(0) == 0)
-    def _():
-        factor(gram_ref, store)
-        factor_ref[...] = turned[...].T
-
-    both = lax.dot_general(
-        filtered_ref[...],
-        split[...].astype(jnp.bfloat16),
-        (((1,), (1,)), ((), ())),
-        preferred_element_type=jnp.float32,
-    )
-    basis_ref[...] = both[:, :size] + both[:, size:]
+    factor(gram_ref, store)
+    load.wait()
+    both_parts = split[...].astype(jnp.bfloat16)
+    stores = []
+    for index, (start, width) in enumerate(spans):
+        rows = pl.ds(start, min(width, basis_ref.shape[0] - start))
+        both = lax.dot_general(
+            filtered_ref[rows, :],
+            both_parts,
+            (((1,), (1,)), ((), ())),
+            preferred_element_type=jnp.float32,
+        )
+        basis_ref[rows, :] = both[:, :size] + both[:, size:]
+        copy = pltpu.make_async_copy(
+            basis_ref.at[rows], basis_hbm.at[rows], store_sem.at[index]
+        )
+        copy.start()
+        stores.append(copy)
+        if index == 0:
+            factor_ref[...] = turned[...].T
+            copy = pltpu.make_async_copy(factor_ref, factor_hbm, store_sem.at[len(spans)])
+            copy.start()
+            stores.append(copy)
+    for copy in stores:
+        copy.wait()
 
 
 def paired_body(thermal_anomaly, smoothing_coefs):
@@ -342,10 +371,10 @@
     total = 2 * hours
     half = sites // 2
     tiles = pl.cdiv(half, LANES)
-    step = pl.cdiv(tiles, CHUNKS)
-    spans = [
-        (t * LANES, min(step, tiles - t) * LANES) for t in range(0, tiles, step)
-    ]
+    edge = max(1, tiles // (2 * CHUNKS))
+    step = max(1, pl.cdiv(tiles - 2 * edge, CHUNKS - 2))
+    cuts = [0, *range(edge, max(edge, tiles - edge), step), max(edge, tiles - edge), tiles]
+    spans = [(a * LANES, (b - a) * LANES) for a, b in zip(cuts, cuts[1:]) if b > a]
     padded = tiles * LANES
     group = PLANE * 2
     lines = lax.axis_size("space") // PLANE
@@ -387,26 +416,23 @@
         name="gather_gram",
     )(thermal_anomaly, smoothing_coefs[: total].reshape(1, total))
 
-    width = step * LANES
     points = sites * lax.axis_size("space")
     basis, lower = pl.pallas_call(
-        functools.partial(basis_kernel, points),
-        grid=(pl.cdiv(half, width),),
+        functools.partial(basis_kernel, points, spans),
         out_shape=(
             jax.ShapeDtypeStruct((half, total), jnp.float32),
             jax.ShapeDtypeStruct((total, total), jnp.float32),
         ),
-        in_specs=[
-            pl.BlockSpec((total, total), lambda i: (0, 0)),
-            pl.BlockSpec((width, total), lambda i: (i, 0)),
-        ],
-        out_specs=(
-            pl.BlockSpec((width, total), lambda i: (i, 0)),
-            pl.BlockSpec((total, total), lambda i: (0, 0)),
-        ),
+        in_specs=[vmem, anywhere],
+        out_specs=(anywhere, anywhere),
         scratch_shapes=[
+            pltpu.VMEM((padded, total), jnp.bfloat16),
+            pltpu.VMEM((half, total), jnp.float32),
+            pltpu.VMEM((total, total), jnp.float32),
             pltpu.VMEM((2 * total, total), jnp.float32),
             pltpu.VMEM((total, total), jnp.float32),
+            dma,
+            dma((len(spans) + 1,)),
         ],
         name="factor_basis",
     )(gram, filtered)

time: 41.6 us -> 40.4 us (0.971)
  Pallas kernels: 40.7 us -> 39.5 us
    pallas_call x1, Pallas kernels: 9.75 us -> 8.62 us  [paired_body(): pl.pallas_call(functools.partial(basis_kernel, points, spans), out_shape=...]
where the time goes in v4:
time: 40.4 us; the launch traced here: 40.1 us
  Pallas kernels  39.5 us (98%)
  between operations  0.64 us (2%)
    pallas_call x1, Pallas kernels, paired_body(): pl.pallas_call(functools.partial(gather_kernel, spans), out_shape=(jax.Sh...  30.9 us
    pallas_call x1, Pallas kernels, paired_body(): pl.pallas_call(functools.partial(basis_kernel, points, spans), out_shape=...  8.62 us

profile of v4, /device:TPU:0, one launch (start us, length us, event | category | flops | bytes accessed | tf_op | source)
XLA Modules:
  0.0 40.1 jit_solution(9529029859832378064)
XLA Ops:
  0.6 30.9 %gather_gram.1 = (bf16[4480,128]{1,0:T(8,128)(2,1)}, f32[128,128]{1,0:T(8,128)}) custom-call(bf16[64,8768]{1,0:T(8,128)(2,1)} %x_hbm.1, f32[1,128]{1,0:T(1,128)} %bitcast.2), custom_call_target="tpu_custom_call" | custom-call | tf_op jit(solution)/shard_map/gather_gram/pallas_call | solution.py:385
  31.5 8.6 %factor_basis.1 = (f32[4384,128]{1,0:T(8,128)}, f32[128,128]{1,0:T(8,128)}) custom-call(f32[128,128]{1,0:T(8,128)} %get-tuple-element.6.gram_ref, bf16[4480,128]{1,0:T(8,128)(2,1)} %get-tuple-element.7.filtered_hbm), custom_call_target="tpu_custom_call" | custom-call | tf_op jit(solution)/shard_map/factor_basis/pallas_call | solution.py:420

commit v5 on v4

--- a/solution.py
+++ b/solution.py
@@ -13,6 +13,7 @@
 PLANE = 4
 CHUNKS = 5
 SLABS = 4
+GRANT = 16 * 2**20
 MESH = pl.DeviceIdType.MESH
 
 
@@ -388,7 +389,7 @@
             jax.ShapeDtypeStruct((padded, total), jnp.bfloat16),
             jax.ShapeDtypeStruct((total, total), jnp.float32),
         ),
-        in_specs=[anywhere, anywhere],
+        in_specs=[pl.BlockSpec(memory_space=pltpu.HBM)] * 2,
         out_specs=(anywhere, vmem),
         scratch_shapes=[
             pltpu.VMEM((hours, sites), jnp.bfloat16),
@@ -412,7 +413,9 @@
             dma((group - 1,)),
             dma((group - 1,)),
         ],
-        compiler_params=pltpu.CompilerParams(collective_id=0, has_side_effects=True),
+        compiler_params=pltpu.CompilerParams(
+            collective_id=0, has_side_effects=True, vmem_limit_bytes=GRANT
+        ),
         name="gather_gram",
     )(thermal_anomaly, smoothing_coefs[: total].reshape(1, total))
 
@@ -434,6 +437,7 @@
             dma,
             dma((len(spans) + 1,)),
         ],
+        compiler_params=pltpu.CompilerParams(vmem_limit_bytes=GRANT),
         name="factor_basis",
     )(gram, filtered)
     return basis.T, lower

time: 40.4 us -> 40.1 us (level)
  Pallas kernels: 39.5 us -> 37.3 us
  local copies, waits for them, and re-layouts: 0 us -> 1.9 us
    unnamed x0 -> x4, local copies, waits for them, and re-layouts: none -> 1.9 us
    pallas_call x1, Pallas kernels: 8.62 us -> 6.82 us  [paired_body(): pl.pallas_call(functools.partial(basis_kernel, points, spans), out_shape=...]
where the time goes in v5:
time: 40.1 us; the launch traced here: 39.9 us
  Pallas kernels  37.3 us (93%)
  local copies, waits for them, and re-layouts  1.9 us (5%)
  between operations  0.65 us (2%)
    pallas_call x1, Pallas kernels, paired_body(): pl.pallas_call(functools.partial(gather_kernel, spans), out_shape=(jax.Sh...  30.5 us
    pallas_call x1, Pallas kernels, paired_body(): pl.pallas_call(functools.partial(basis_kernel, points, spans), out_shape=...  6.82 us
    unnamed x4, local copies, waits for them, and re-layouts  1.9 us

profile of v5, /device:TPU:0, one launch (start us, length us, event | category | flops | bytes accessed | tf_op | source)
XLA Modules:
  0.0 39.9 jit_solution(13729652790720411013)
XLA Ops:
  0.6 0.0 copy-start
  0.6 1.2 %copy-done = bf16[64,8768]{1,0:T(8,128)(2,1)S(1)} copy-done((bf16[64,8768]{1,0:T(8,128)(2,1)S(1)}, bf16[64,8768]{1,0:T(8,128)(2,1)}, u32[]{:S(2)}) %copy-start) | copy-done | bytes 1122328
  1.9 0.0 copy-start.1
  1.9 0.7 %copy-done.1 = f32[128]{0:T(128)S(1)} copy-done((f32[128]{0:T(128)S(1)}, f32[128]{0:T(128)}, u32[]{:S(2)}) %copy-start.1) | copy-done | bytes 536
  2.5 30.5 %gather_gram.1 = (bf16[4480,128]{1,0:T(8,128)(2,1)S(1)}, f32[128,128]{1,0:T(8,128)S(1)}) custom-call(bf16[64,8768]{1,0:T(8,128)(2,1)S(1)} %copy-done, f32[1,128]{1,0:T(1,128)S(1)} %bitcast.2), custom_call_target="tpu_custom_call" | custom-call | tf_op jit(solution)/shard_map/gather_gram/pallas_call | solution.py:386
  33.1 6.8 %factor_basis.1 = (f32[4384,128]{1,0:T(8,128)}, f32[128,128]{1,0:T(8,128)}) custom-call(f32[128,128]{1,0:T(8,128)S(1)} %get-tuple-element.6.gram_ref, bf16[4480,128]{1,0:T(8,128)(2,1)S(1)} %get-tuple-element.7.filtered_hbm), custom_call_target="tpu_custom_call" | custom-call | tf_op jit(solution)/shard_map/factor_basis/pallas_call | solution.py:423
Async XLA Ops:
  0.6 1.3 %copy-start = (bf16[64,8768]{1,0:T(8,128)(2,1)S(1)}, bf16[64,8768]{1,0:T(8,128)(2,1)}, u32[]{:S(2)}) copy-start(bf16[64,8768]{1,0:T(8,128)(2,1)} %x_hbm.1) | copy-start | bytes 3366916
  1.9 0.7 %copy-start.1 = (f32[128]{0:T(128)S(1)}, f32[128]{0:T(128)}, u32[]{:S(2)}) copy-start(f32[128]{0:T(128)} %param.3) | copy-start | bytes 1540
